TPU v7x, 512 devices: a whole 4x8x8 slice. The times are simulated.
512 devices in a mesh: ctx: 64 (over x, z_lo, y), head: 8 (over z_hi, core).
Axes of the slice: x: 4, y: 8, z: 8 (z_hi: 4, z_lo: 2; z = z_hi * 2 + z_lo), core: 2. Of those that a mesh axis runs over, the one named last changes fastest.
Arguments:
- queries: bfloat16 [16384, 4096], P('ctx', 'head'), may hold values from -12 to 12
- keys: bfloat16 [16384, 4096], P('ctx', 'head'), may hold values from -4 to 4
- values: bfloat16 [16384, 4096], P('ctx', 'head'), may hold values from -6 to 6
- pool_weight: bfloat16 [512, 256], P('ctx'), may hold values from -0.375 to 0.375
- out_weight: bfloat16 [4096, 4096], P('head', 'ctx'), may hold values from -0.09375 to 0.09375
- pattern: int32 [128, 7], replicated, may hold values from 0 to 127, as said below
Outputs:
- mixed: bfloat16 [16384, 4096], P('ctx', 'head')
Inputs may be any that keep to these rules, and one draw needn't show every extreme that they name: `pattern`: the flat butterfly with the blocks of each shard relabelled: entry (i, b) names a key block that agrees with block i in all bits above b and differs from it in bit b. For b < 1 the lower bits are arbitrary. For b >= 1 the bits from 1 to b - 1 equal those of i, and over the 2 query blocks of one aligned group of 2 blocks the lowest 1 bits take each of their 2 values once.
All inputs are finite; a program needn't handle non-finite values.
Results may differ from a plain program's by a relative error of at most 0.019.
Values may be sent and summed in bfloat16 or wider, within the bound.
No kernel may reach another device: no remote copies, remote signals or barrier semaphores. Data moves between devices by JAX's collectives and lax.ppermute only.
A program may use at most 64 MiB of HBM per device.

v0:
```python
import jax
import jax.numpy as jnp
from jax import lax
from jax.sharding import PartitionSpec as P

HEAD_DIMENSION = 128
BLK = 128


def partner_2(x, axis, stride):
    return lax.ppermute(x, axis, [(i, i ^ 1 << stride) for i in range(lax.axis_size(axis))])


def merge_scores(running, scores, value_set, einsum_form):
    old_max, row_sum, weighted = running
    row_max = jnp.maximum(old_max, jnp.max(scores, axis=-1))
    weights = jnp.exp(scores - row_max[..., None])
    rescale = jnp.exp(old_max - row_max)
    row_sum = row_sum * rescale + jnp.sum(weights, axis=-1)
    weighted = weighted * rescale[..., None] + jnp.einsum(
        einsum_form, weights.astype(jnp.bfloat16), value_set, preferred_element_type=jnp.float32
    )
    return (row_max, row_sum, weighted)


def on_device(queries, keys, values, pool_weight, out_weight, pattern):
    tok_rows, col_width = queries.shape
    local_heads = col_width // HEAD_DIMENSION
    block_count = tok_rows // BLK
    local_bits = block_count.bit_length() - 1
    remote_bits = lax.axis_size("ctx").bit_length() - 1
    score_scale = HEAD_DIMENSION ** (-0.5)
    own_index = lax.axis_index("ctx")
    own_rows = lax.dynamic_slice_in_dim(pattern, own_index * block_count, block_count, 0)
    query_blk = queries.reshape(block_count, BLK, local_heads, HEAD_DIMENSION)
    key_rows = keys.reshape(block_count, BLK, col_width)
    value_rows = values.reshape(block_count, BLK, col_width)
    running = (
        jnp.full((block_count, local_heads, BLK), -jnp.inf, jnp.float32),
        jnp.zeros((block_count, local_heads, BLK), jnp.float32),
        jnp.zeros((block_count, local_heads, BLK, HEAD_DIMENSION), jnp.float32),
    )
    near_index = jnp.concatenate(
        [
            jnp.arange(block_count, dtype=jnp.int32)[:, None],
            own_rows[:, :local_bits] - own_index * block_count,
        ],
        axis=1,
    )
    near_keys = jnp.take(key_rows, near_index, axis=0).reshape(
        block_count, -1, local_heads, HEAD_DIMENSION
    )
    near_values = jnp.take(value_rows, near_index, axis=0).reshape(
        block_count, -1, local_heads, HEAD_DIMENSION
    )
    scores = (
        jnp.einsum("bqhd,bkhd->bhqk", query_blk, near_keys, preferred_element_type=jnp.float32)
        * score_scale
    )
    running = merge_scores(running, scores, near_values, "bhqk,bkhd->bhqd")
    pooled_landmark_keys = jnp.dot(pool_weight, keys, preferred_element_type=jnp.float32).astype(
        jnp.bfloat16
    )
    pooled_landmark_values = jnp.dot(
        pool_weight, values, preferred_element_type=jnp.float32
    ).astype(jnp.bfloat16)
    piece_keys = lax.all_gather(pooled_landmark_keys, "ctx", axis=0, tiled=True).reshape(
        -1, local_heads, HEAD_DIMENSION
    )
    piece_values = lax.all_gather(pooled_landmark_values, "ctx", axis=0, tiled=True).reshape(
        -1, local_heads, HEAD_DIMENSION
    )
    mark_scores = (
        jnp.einsum("bqhd,khd->bhqk", query_blk, piece_keys, preferred_element_type=jnp.float32)
        * score_scale
    )
    running = merge_scores(running, mark_scores, piece_values, "bhqk,khd->bhqd")
    for level in range(remote_bits):
        partner = jnp.bitwise_xor(own_index, 1 << level)
        wanted = own_rows[:, local_bits + level] - partner * block_count
        recv_keys, recv_values = partner_2((key_rows, value_rows), "ctx", level)
        far_keys = jnp.take(recv_keys, wanted, axis=0)
        far_values = jnp.take(recv_values, wanted, axis=0)
        far_scores = (
            jnp.einsum(
                "bqhd,bkhd->bhqk",
                query_blk,
                far_keys.reshape(block_count, BLK, local_heads, HEAD_DIMENSION),
                preferred_element_type=jnp.float32,
            )
            * score_scale
        )
        running = merge_scores(
            running,
            far_scores,
            far_values.reshape(block_count, BLK, local_heads, HEAD_DIMENSION),
            "bhqk,bkhd->bhqd",
        )
    row_max, row_sum, weighted = running
    attended = (
        (weighted / row_sum[..., None])
        .transpose(0, 2, 1, 3)
        .reshape(tok_rows, col_width)
        .astype(jnp.bfloat16)
    )
    partial_value = jnp.dot(
        attended,
        lax.all_gather(out_weight, "ctx", axis=1, tiled=True),
        preferred_element_type=jnp.float32,
    )
    return lax.psum_scatter(
        partial_value.astype(jnp.bfloat16), "head", scatter_dimension=1, tiled=True
    )


def solution(mesh):
    in_specs = (
        P("ctx", "head"),
        P("ctx", "head"),
        P("ctx", "head"),
        P("ctx", None),
        P("head", "ctx"),
        P(),
    )
    out_specs = P("ctx", "head")
    return jax.shard_map(
        on_device, mesh=mesh, in_specs=in_specs, out_specs=out_specs, check_vma=False
    )
```

profile of v0, /device:TPU:28, one launch (start us, length us, event | category | flops | bytes accessed | tf_op | source)
XLA Modules:
  0.0 505.4 jit_solution(15221089490795249946)
XLA Ops:
  6.5 5.2 %collective-permute-start.4 = (bf16[2,128,512]{2,1,0:T(8,128)(2,1)}, bf16[2,128,512]{2,1,0:T(8,128)(2,1)}, u32[]{:S(2)}, u32[]{:S(2)}) collective-permute-start(bf16[2,128,512]{2,1,0:T(8,128)(2,1)} %bitcast.272), channel_id=1, source_target_pairs={{0,32},{8,40},{16,48},{24,56},{32,0},{40,8},{48,16},{56,24},{64,96... | collective-permute-start | bytes 786440 | tf_op jit(solution)/shard_map/ppermute | solution.py:11
  11.7 4.3 collective-permute-start.6
  16.0 4.7 collective-permute-start.5
  22.7 2.4 collective-permute-start
  29.6 137.3 %all_gather.9 = bf16[512,512]{1,0:T(8,128)(2,1)S(1)} all-gather(bf16[8,512]{1,0:T(8,128)(2,1)S(1)} %convolution_convert_fusion.2), channel_id=1, replica_groups=mesh['ctx'=64,'head'=8] {'ctx'}, dimensions={0}, use_global_device_ids=true | all-gather | bytes 532480 | tf_op jit(solution)/shard_map/all_gather | solution.py:67
  170.1 135.2 %all_gather.10 = bf16[512,512]{1,0:T(8,128)(2,1)S(1)} all-gather(bf16[8,512]{1,0:T(8,128)(2,1)S(1)} %convolution_convert_fusion.1), channel_id=1, replica_groups=mesh['ctx'=64,'head'=8] {'ctx'}, dimensions={0}, use_global_device_ids=true | all-gather | bytes 532480 | tf_op jit(solution)/shard_map/all_gather | solution.py:70
  307.9 2.3 collective-permute-start.1
  310.2 2.2 gather_fusion.6
  312.4 6.4 %collective-permute-start.2 = (bf16[2,128,512]{2,1,0:T(8,128)(2,1)}, bf16[2,128,512]{2,1,0:T(8,128)(2,1)}, u32[]{:S(2)}, u32[]{:S(2)}) collective-permute-start(bf16[2,128,512]{2,1,0:T(8,128)(2,1)} %bitcast.276), channel_id=1, source_target_pairs={{0,16},{8,24},{16,0},{24,8},{32,48},{40,56},{48,32},{56,40},{64,80... | collective-permute-start | bytes 786440 | tf_op jit(solution)/shard_map/ppermute | solution.py:11
  318.8 2.2 gather_fusion.7
  323.0 2.2 gather_fusion.8
  325.2 21.4 %collective-permute-start.8 = (bf16[2,128,512]{2,1,0:T(8,128)(2,1)}, bf16[2,128,512]{2,1,0:T(8,128)(2,1)}, u32[]{:S(2)}, u32[]{:S(2)}) collective-permute-start(bf16[2,128,512]{2,1,0:T(8,128)(2,1)} %bitcast.277), channel_id=1, source_target_pairs={{0,128},{8,136},{16,144},{24,152},{32,160},{40,168},{48,176},{56,1... | collective-permute-start | bytes 786440 | tf_op jit(solution)/shard_map/ppermute | solution.py:11
  346.6 2.2 gather_fusion.9
  348.9 2.3 broadcast_select_fusion.6
  356.7 2.2 gather_fusion.2
  358.9 24.6 %collective-permute-start.11 = (bf16[2,128,512]{2,1,0:T(8,128)(2,1)}, bf16[2,128,512]{2,1,0:T(8,128)(2,1)}, u32[]{:S(2)}, u32[]{:S(2)}) collective-permute-start(bf16[2,128,512]{2,1,0:T(8,128)(2,1)} %bitcast.4), channel_id=1, source_target_pairs={{0,256},{8,264},{16,272},{24,280},{32,288},{40,296},{48,304},{56,3... | collective-permute-start | bytes 786440 | tf_op jit(solution)/shard_map/ppermute | solution.py:11
  387.8 2.2 gather_fusion.4
  390.0 2.2 gather_fusion.5
  392.2 2.3 broadcast_select_fusion.10
  402.5 2.2 gather_fusion.13
  404.7 2.2 gather_fusion.12
  407.0 2.3 broadcast_select_fusion.3
  442.1 4.8 convolution_convert_fusion
  447.0 51.6 %reduce-scatter.2.cloned.1.call-done = bf16[256,512]{1,0:T(8,128)(2,1)} async-done(((bf16[256,4096]{1,0:T(8,128)(2,1)}), bf16[256,512]{1,0:T(8,128)(2,1)}) %reduce-scatter.2.cloned.1.call-update) | async-done | bytes 262160 | tf_op jit(solution)/shard_map/reduce_scatter | solution.py:111
  (131 shorter events, 64.4 us)
Async XLA Ops:
  6.5 22.8 %copy-start = (bf16[8,256]{1,0:T(8,128)(2,1)S(1)}, bf16[8,256]{1,0:T(8,128)(2,1)}, u32[]{:S(2)}) copy-start(bf16[8,256]{1,0:T(8,128)(2,1)} %param.13) | copy-start | bytes 12292
  6.5 22.8 %copy-start.7 = (bf16[256,512]{1,0:T(8,128)(2,1)S(1)}, bf16[256,512]{1,0:T(8,128)(2,1)}, u32[]{:S(2)}) copy-start(bf16[256,512]{1,0:T(8,128)(2,1)} %param.11) | copy-start | bytes 786436
  6.5 435.6 %all-gather.2.cloned.1.call-start = ((), (), s32[]{:S(2)}) async-start(), calls=%async_computation.1 | async-start | bytes 4259840 | tf_op jit(solution)/shard_map/all_gather | solution.py:108
  6.5 301.3 %collective-permute-start.4 = (bf16[2,128,512]{2,1,0:T(8,128)(2,1)}, bf16[2,128,512]{2,1,0:T(8,128)(2,1)}, u32[]{:S(2)}, u32[]{:S(2)}) collective-permute-start(bf16[2,128,512]{2,1,0:T(8,128)(2,1)} %bitcast.272), channel_id=1, source_target_pairs={{0,32},{8,40},{16,48},{24,56},{32,0},{40,8},{48,16},{56,24},{64,96... | collective-permute-start | bytes 786440 | tf_op jit(solution)/shard_map/ppermute | solution.py:11
  11.7 309.3 %collective-permute-start.6 = (bf16[2,128,512]{2,1,0:T(8,128)(2,1)}, bf16[2,128,512]{2,1,0:T(8,128)(2,1)}, u32[]{:S(2)}, u32[]{:S(2)}) collective-permute-start(bf16[2,128,512]{2,1,0:T(8,128)(2,1)} %bitcast.273), channel_id=1, source_target_pairs={{0,64},{8,72},{16,80},{24,88},{32,96},{40,104},{48,112},{56,120},{... | collective-permute-start | bytes 786440 | tf_op jit(solution)/shard_map/ppermute | solution.py:11
  16.0 296.4 %collective-permute-start.5 = (bf16[2,128,512]{2,1,0:T(8,128)(2,1)}, bf16[2,128,512]{2,1,0:T(8,128)(2,1)}, u32[]{:S(2)}, u32[]{:S(2)}) collective-permute-start(bf16[2,128,512]{2,1,0:T(8,128)(2,1)} %bitcast.4), channel_id=1, source_target_pairs={{0,32},{8,40},{16,48},{24,56},{32,0},{40,8},{48,16},{56,24},{64,96... | collective-permute-start | bytes 786440 | tf_op jit(solution)/shard_map/ppermute | solution.py:11
  20.7 304.5 %collective-permute-start.7 = (bf16[2,128,512]{2,1,0:T(8,128)(2,1)}, bf16[2,128,512]{2,1,0:T(8,128)(2,1)}, u32[]{:S(2)}, u32[]{:S(2)}) collective-permute-start(bf16[2,128,512]{2,1,0:T(8,128)(2,1)} %bitcast.4), channel_id=1, source_target_pairs={{0,64},{8,72},{16,80},{24,88},{32,96},{40,104},{48,112},{56,120},{... | collective-permute-start | bytes 786440 | tf_op jit(solution)/shard_map/ppermute | solution.py:11
  22.7 332.1 %collective-permute-start = (bf16[2,128,512]{2,1,0:T(8,128)(2,1)}, bf16[2,128,512]{2,1,0:T(8,128)(2,1)}, u32[]{:S(2)}, u32[]{:S(2)}) collective-permute-start(bf16[2,128,512]{2,1,0:T(8,128)(2,1)} %bitcast.274), channel_id=1, source_target_pairs={{0,8},{8,0},{16,24},{24,16},{32,40},{40,32},{48,56},{56,48},{64,72... | collective-permute-start | bytes 786440 | tf_op jit(solution)/shard_map/ppermute | solution.py:11
  25.1 473.5 %reduce-scatter.2.cloned.1.call-start = ((), (), s32[]{:S(2)}) async-start(), calls=%async_computation.2 | async-start | bytes 2359296 | tf_op jit(solution)/shard_map/reduce_scatter | solution.py:111
  27.6 139.3 %copy-start.20 = (bf16[256,512]{1,0:T(8,128)(2,1)S(1)}, bf16[256,512]{1,0:T(8,128)(2,1)}, u32[]{:S(2)}) copy-start(bf16[256,512]{1,0:T(8,128)(2,1)} %param.10) | copy-start | bytes 786436
  307.9 51.0 %collective-permute-start.1 = (bf16[2,128,512]{2,1,0:T(8,128)(2,1)}, bf16[2,128,512]{2,1,0:T(8,128)(2,1)}, u32[]{:S(2)}, u32[]{:S(2)}) collective-permute-start(bf16[2,128,512]{2,1,0:T(8,128)(2,1)} %bitcast.4), channel_id=1, source_target_pairs={{0,8},{8,0},{16,24},{24,16},{32,40},{40,32},{48,56},{56,48},{64,72... | collective-permute-start | bytes 786440 | tf_op jit(solution)/shard_map/ppermute | solution.py:11
  312.4 73.3 %collective-permute-start.2 = (bf16[2,128,512]{2,1,0:T(8,128)(2,1)}, bf16[2,128,512]{2,1,0:T(8,128)(2,1)}, u32[]{:S(2)}, u32[]{:S(2)}) collective-permute-start(bf16[2,128,512]{2,1,0:T(8,128)(2,1)} %bitcast.276), channel_id=1, source_target_pairs={{0,16},{8,24},{16,0},{24,8},{32,48},{40,56},{48,32},{56,40},{64,80... | collective-permute-start | bytes 786440 | tf_op jit(solution)/shard_map/ppermute | solution.py:11
  321.1 69.0 %collective-permute-start.3 = (bf16[2,128,512]{2,1,0:T(8,128)(2,1)}, bf16[2,128,512]{2,1,0:T(8,128)(2,1)}, u32[]{:S(2)}, u32[]{:S(2)}) collective-permute-start(bf16[2,128,512]{2,1,0:T(8,128)(2,1)} %bitcast.4), channel_id=1, source_target_pairs={{0,16},{8,24},{16,0},{24,8},{32,48},{40,56},{48,32},{56,40},{64,80... | collective-permute-start | bytes 786440 | tf_op jit(solution)/shard_map/ppermute | solution.py:11
  325.2 72.9 %collective-permute-start.8 = (bf16[2,128,512]{2,1,0:T(8,128)(2,1)}, bf16[2,128,512]{2,1,0:T(8,128)(2,1)}, u32[]{:S(2)}, u32[]{:S(2)}) collective-permute-start(bf16[2,128,512]{2,1,0:T(8,128)(2,1)} %bitcast.277), channel_id=1, source_target_pairs={{0,128},{8,136},{16,144},{24,152},{32,160},{40,168},{48,176},{56,1... | collective-permute-start | bytes 786440 | tf_op jit(solution)/shard_map/ppermute | solution.py:11
  354.8 45.6 %collective-permute-start.9 = (bf16[2,128,512]{2,1,0:T(8,128)(2,1)}, bf16[2,128,512]{2,1,0:T(8,128)(2,1)}, u32[]{:S(2)}, u32[]{:S(2)}) collective-permute-start(bf16[2,128,512]{2,1,0:T(8,128)(2,1)} %bitcast.4), channel_id=1, source_target_pairs={{0,128},{8,136},{16,144},{24,152},{32,160},{40,168},{48,176},{56,1... | collective-permute-start | bytes 786440 | tf_op jit(solution)/shard_map/ppermute | solution.py:11
  358.9 43.6 %collective-permute-start.11 = (bf16[2,128,512]{2,1,0:T(8,128)(2,1)}, bf16[2,128,512]{2,1,0:T(8,128)(2,1)}, u32[]{:S(2)}, u32[]{:S(2)}) collective-permute-start(bf16[2,128,512]{2,1,0:T(8,128)(2,1)} %bitcast.4), channel_id=1, source_target_pairs={{0,256},{8,264},{16,272},{24,280},{32,288},{40,296},{48,304},{56,3... | collective-permute-start | bytes 786440 | tf_op jit(solution)/shard_map/ppermute | solution.py:11
  385.7 19.1 %collective-permute-start.10 = (bf16[2,128,512]{2,1,0:T(8,128)(2,1)}, bf16[2,128,512]{2,1,0:T(8,128)(2,1)}, u32[]{:S(2)}, u32[]{:S(2)}) collective-permute-start(bf16[2,128,512]{2,1,0:T(8,128)(2,1)} %bitcast.278), channel_id=1, source_target_pairs={{0,256},{8,264},{16,272},{24,280},{32,288},{40,296},{48,304},{56,3... | collective-permute-start | bytes 786440 | tf_op jit(solution)/shard_map/ppermute | solution.py:11
  412.9 4.3 copy-start.17
  412.9 5.4 %copy-start.16 = (bf16[2,128,512]{1,2,0:T(8,128)(2,1)S(1)}, bf16[2,128,512]{1,2,0:T(8,128)(2,1)}, u32[]{:S(2)}) copy-start(bf16[2,128,512]{1,2,0:T(8,128)(2,1)} %copy.203) | copy-start | bytes 786436
  412.9 6.6 %copy-start.19 = (bf16[2,128,512]{1,2,0:T(8,128)(2,1)S(1)}, bf16[2,128,512]{1,2,0:T(8,128)(2,1)}, u32[]{:S(2)}) copy-start(bf16[2,128,512]{1,2,0:T(8,128)(2,1)} %copy.233) | copy-start | bytes 786436
  415.0 5.5 %copy-start.18 = (bf16[2,128,512]{1,2,0:T(8,128)(2,1)S(1)}, bf16[2,128,512]{1,2,0:T(8,128)(2,1)}, u32[]{:S(2)}) copy-start(bf16[2,128,512]{1,2,0:T(8,128)(2,1)} %copy.227) | copy-start | bytes 786436
  431.9 4.7 copy-start.6
  431.9 4.8 copy-start.4
  437.3 1.5 copy-start.12
  (11 other events, 13.0 us)
Sparse Core Ops, SparseCore 0:
  25.2 272.9 all-gather.1
  447.1 51.3 reduce-scatter.1
where the time goes:
time: 507 us; the launch traced here: 505 us
  blocking collectives  273 us (54%)
  starting transfers between devices  79.1 us (16%)
  local copies, waits for them, and re-layouts  55.9 us (11%)
  waiting for transfers between devices  51.6 us (10%)
  matrix products  19.7 us (4%)
  between operations  13.9 us (3%)
  other arithmetic  12.6 us (2%)
    all_gather x1, blocking collectives, on_device(): lax.all_gather(pooled_landmark_keys, 'ctx', axis=0, tiled=True)  137 us
    all_gather x1, blocking collectives, on_device(): lax.all_gather(pooled_landmark_values, 'ctx', axis=0, tiled=True)  135 us
    ppermute x12, starting transfers between devices, partner_2(): lax.ppermute(x, axis, [(i, i ^ 1 << stride) for i in range(lax.axis_size(...  79.1 us
    reduce_scatter x1, waiting for transfers between devices, on_device(): lax.psum_scatter(partial_value.astype(jnp.bfloat16), 'head', scatter_dime...  51.6 us
    gather x6, local copies, waits for them, and re-layouts, on_device(): far_keys = jnp.take(recv_keys, wanted, axis=0)  13.3 us
    gather x6, local copies, waits for them, and re-layouts, on_device(): far_values = jnp.take(recv_values, wanted, axis=0)  13.3 us
    select_n x6, local copies, waits for them, and re-layouts, on_device(): far_keys = jnp.take(recv_keys, wanted, axis=0)  10.7 us
  transfers between devices with their start and end apart: 14, of which 1 were waited for; matrix products, arithmetic and copies ran while one was open for 16% of the time, Pallas kernels for 0%

commit v1 on v0

--- a/solution.py
+++ b/solution.py
@@ -5,6 +5,11 @@
 
 HEAD_DIMENSION = 128
 BLK = 128
+
+
+def all_by_exchange(value, name, dim):
+    repeated = jnp.stack([value] * lax.axis_size(name))
+    return jnp.concatenate(lax.all_to_all(repeated, name, 0, 0), axis=dim)
 
 
 def partner_2(x, axis, stride):
@@ -64,7 +69,7 @@
     pooled_landmark_values = jnp.dot(
         pool_weight, values, preferred_element_type=jnp.float32
     ).astype(jnp.bfloat16)
-    piece_keys = lax.all_gather(pooled_landmark_keys, "ctx", axis=0, tiled=True).reshape(
+    piece_keys = all_by_exchange(pooled_landmark_keys, "ctx", 0).reshape(
         -1, local_heads, HEAD_DIMENSION
     )
     piece_values = lax.all_gather(pooled_landmark_values, "ctx", axis=0, tiled=True).reshape(

time: 507 us -> 410 us (0.81)
  the two profiles are of different devices: /device:TPU:28 before, /device:TPU:4 now
where the time goes in v1:
time: 410 us; the launch traced here: 409 us
  blocking collectives  138 us (34%)
  waiting for transfers between devices  120 us (29%)
  starting transfers between devices  71.1 us (17%)
  local copies, waits for them, and re-layouts  41.8 us (10%)
  matrix products  17.5 us (4%)
  between operations  14 us (3%)
  other arithmetic  5.58 us (1%)
    all_gather x1, blocking collectives, on_device(): lax.all_gather(pooled_landmark_values, 'ctx', axis=0, tiled=True)  138 us
    reduce_scatter x1, waiting for transfers between devices, on_device(): lax.psum_scatter(partial_value.astype(jnp.bfloat16), 'head', scatter_dime...  75.9 us
    ppermute x12, starting transfers between devices, partner_2(): lax.ppermute(x, axis, [(i, i ^ 1 << stride) for i in range(lax.axis_size(...  59.6 us
    all_gather x1, waiting for transfers between devices, on_device(): lax.all_gather(out_weight, 'ctx', axis=1, tiled=True)  43.6 us
    all_to_all x1, starting transfers between devices, all_by_exchange(): return jnp.concatenate(lax.all_to_all(repeated, name, 0, 0), axis=dim)  11.5 us
    gather x6, local copies, waits for them, and re-layouts, on_device(): far_values = jnp.take(recv_values, wanted, axis=0)  10.2 us
    select_n x6, local copies, waits for them, and re-layouts, on_device(): far_values = jnp.take(recv_values, wanted, axis=0)  8.89 us
    gather x6, local copies, waits for them, and re-layouts, on_device(): far_keys = jnp.take(recv_keys, wanted, axis=0)  8.84 us
  transfers between devices with their start and end apart: 15, of which 2 were waited for; matrix products, arithmetic and copies ran while one was open for 15% of the time, Pallas kernels for 0%

profile of v1, /device:TPU:4, one launch (start us, length us, event | category | flops | bytes accessed | tf_op | source)
XLA Modules:
  0.0 408.5 jit_solution(2294172362412639087)
XLA Ops:
  6.5 7.9 %collective-permute-start.4 = (bf16[2,128,512]{2,1,0:T(8,128)(2,1)}, bf16[2,128,512]{2,1,0:T(8,128)(2,1)}, u32[]{:S(2)}, u32[]{:S(2)}) collective-permute-start(bf16[2,128,512]{2,1,0:T(8,128)(2,1)} %bitcast.279), channel_id=1, source_target_pairs={{0,32},{8,40},{16,48},{24,56},{32,0},{40,8},{48,16},{56,24},{64,96... | collective-permute-start | bytes 786440 | tf_op jit(solution)/shard_map/ppermute | solution.py:16
  14.4 4.3 %collective-permute-start.6 = (bf16[2,128,512]{2,1,0:T(8,128)(2,1)}, bf16[2,128,512]{2,1,0:T(8,128)(2,1)S(1)}, u32[]{:S(2)}, u32[]{:S(2)}) collective-permute-start(bf16[2,128,512]{2,1,0:T(8,128)(2,1)} %bitcast.280), channel_id=1, source_target_pairs={{0,64},{8,72},{16,80},{24,88},{32,96},{40,104},{48,112},{56,120},{... | collective-permute-start | bytes 786440 | tf_op jit(solution)/shard_map/ppermute | solution.py:16
  18.7 2.0 collective-permute-start.5
  20.7 1.9 collective-permute-start.7
  22.6 3.5 collective-permute-start
  28.1 11.5 %all-to-all-start = ((bf16[64,8,512]{2,1,0:T(8,128)(2,1)}), bf16[64,8,512]{2,1,0:T(8,128)(2,1)}, u32[]{:S(2)}, u32[]{:S(2)}) async-start(bf16[64,8,512]{2,1,0:T(8,128)(2,1)} %stack.2), calls=%async_computation | async-start | bytes 1048576 | tf_op jit(solution)/shard_map/all_to_all | solution.py:12
  45.0 138.2 %all_gather.6 = bf16[512,512]{1,0:T(8,128)(2,1)S(1)} all-gather(bf16[8,512]{1,0:T(8,128)(2,1)S(1)} %convolution_convert_fusion.1), channel_id=1, replica_groups=mesh['ctx'=64,'head'=8] {'ctx'}, dimensions={0}, use_global_device_ids=true | all-gather | bytes 532480 | tf_op jit(solution)/shard_map/all_gather | solution.py:75
  184.7 2.0 collective-permute-start.1
  186.7 1.9 collective-permute-start.2
  191.9 4.8 %collective-permute-start.3 = (bf16[2,128,512]{2,1,0:T(8,128)(2,1)S(1)}, bf16[2,128,512]{2,1,0:T(8,128)(2,1)}, u32[]{:S(2)}, u32[]{:S(2)}) collective-permute-start(bf16[2,128,512]{2,1,0:T(8,128)(2,1)S(1)} %bitcast.276), channel_id=1, source_target_pairs={{0,16},{8,24},{16,0},{24,8},{32,48},{40,56},{48,32},{56,40},{64,80... | collective-permute-start | bytes 786440 | tf_op jit(solution)/shard_map/ppermute | solution.py:16
  197.3 3.3 collective-permute-start.8
  201.2 2.5 collective-permute-start.9
  203.8 23.3 %collective-permute-start.11 = (bf16[2,128,512]{2,1,0:T(8,128)(2,1)S(1)}, bf16[2,128,512]{2,1,0:T(8,128)(2,1)}, u32[]{:S(2)}, u32[]{:S(2)}) collective-permute-start(bf16[2,128,512]{2,1,0:T(8,128)(2,1)S(1)} %bitcast.278), channel_id=1, source_target_pairs={{0,256},{8,264},{16,272},{24,280},{32,288},{40,296},{48,304},{56,3... | collective-permute-start | bytes 786440 | tf_op jit(solution)/shard_map/ppermute | solution.py:16
  227.1 2.1 collective-permute-start.10
  235.1 2.2 gather_fusion.5
  238.9 2.2 gather_fusion.11
  241.1 2.2 gather_fusion.13
  243.3 2.2 gather_fusion.12
  245.9 2.0 broadcast_select_fusion.10
  266.0 2.1 fusion.84
  268.1 2.0 reshape_reshape.3
  277.4 43.6 %all-gather.2.cloned.1.call-done = bf16[512,4096]{0,1:T(8,128)(2,1)} async-done(((bf16[512,64]{0,1:T(8,128)(2,1)}), bf16[512,4096]{0,1:T(8,128)(2,1)}) %all-gather.2.cloned.1.call-update) | async-done | bytes 4194320 | tf_op jit(solution)/shard_map/all_gather | solution.py:113
  321.0 4.8 %convolution_convert_fusion = bf16[256,4096]{1,0:T(8,128)(2,1)} fusion(bf16[512,4096]{0,1:T(8,128)(2,1)} %all-gather.2.cloned.1.call-done, bf16[32,8,4,128]{3,2,1,0:T(4,128)(2,1)S(1)} %bitcast.296), kind=kOutput, calls=%fused_computation.14 | convolution fusion | flops 1074790400 | bytes 6553600 | tf_op jit(solution)/shard_map/dot_general | solution.py:111
  325.8 75.9 %reduce-scatter.2.cloned.1.call-done = bf16[256,512]{1,0:T(8,128)(2,1)} async-done(((bf16[256,4096]{1,0:T(8,128)(2,1)}), bf16[256,512]{1,0:T(8,128)(2,1)}) %reduce-scatter.2.cloned.1.call-update) | async-done | bytes 262160 | tf_op jit(solution)/shard_map/reduce_scatter | solution.py:116
  (131 shorter events, 46.0 us)
Async XLA Ops:
  6.5 19.6 %copy-start = (bf16[8,256]{1,0:T(8,128)(2,1)S(1)}, bf16[8,256]{1,0:T(8,128)(2,1)}, u32[]{:S(2)}) copy-start(bf16[8,256]{1,0:T(8,128)(2,1)} %param.13) | copy-start | bytes 12292
  6.5 34.8 %copy-start.4 = (bf16[256,512]{1,0:T(8,128)(2,1)S(1)}, bf16[256,512]{1,0:T(8,128)(2,1)}, u32[]{:S(2)}) copy-start(bf16[256,512]{1,0:T(8,128)(2,1)} %param.11) | copy-start | bytes 786436
  6.5 35.4 %copy-start.3 = (bf16[256,512]{1,0:T(8,128)(2,1)S(1)}, bf16[256,512]{1,0:T(8,128)(2,1)}, u32[]{:S(2)}) copy-start(bf16[256,512]{1,0:T(8,128)(2,1)} %param.12) | copy-start | bytes 786436
  6.5 178.1 %collective-permute-start.4 = (bf16[2,128,512]{2,1,0:T(8,128)(2,1)}, bf16[2,128,512]{2,1,0:T(8,128)(2,1)}, u32[]{:S(2)}, u32[]{:S(2)}) collective-permute-start(bf16[2,128,512]{2,1,0:T(8,128)(2,1)} %bitcast.279), channel_id=1, source_target_pairs={{0,32},{8,40},{16,48},{24,56},{32,0},{40,8},{48,16},{56,24},{64,96... | collective-permute-start | bytes 786440 | tf_op jit(solution)/shard_map/ppermute | solution.py:16
  14.4 177.5 %collective-permute-start.6 = (bf16[2,128,512]{2,1,0:T(8,128)(2,1)}, bf16[2,128,512]{2,1,0:T(8,128)(2,1)S(1)}, u32[]{:S(2)}, u32[]{:S(2)}) collective-permute-start(bf16[2,128,512]{2,1,0:T(8,128)(2,1)} %bitcast.280), channel_id=1, source_target_pairs={{0,64},{8,72},{16,80},{24,88},{32,96},{40,104},{48,112},{56,120},{... | collective-permute-start | bytes 786440 | tf_op jit(solution)/shard_map/ppermute | solution.py:16
  18.7 168.0 %collective-permute-start.5 = (bf16[2,128,512]{2,1,0:T(8,128)(2,1)}, bf16[2,128,512]{2,1,0:T(8,128)(2,1)}, u32[]{:S(2)}, u32[]{:S(2)}) collective-permute-start(bf16[2,128,512]{2,1,0:T(8,128)(2,1)} %bitcast.272), channel_id=1, source_target_pairs={{0,32},{8,40},{16,48},{24,56},{32,0},{40,8},{48,16},{56,24},{64,96... | collective-permute-start | bytes 786440 | tf_op jit(solution)/shard_map/ppermute | solution.py:16
  20.7 176.6 %collective-permute-start.7 = (bf16[2,128,512]{2,1,0:T(8,128)(2,1)}, bf16[2,128,512]{2,1,0:T(8,128)(2,1)S(1)}, u32[]{:S(2)}, u32[]{:S(2)}) collective-permute-start(bf16[2,128,512]{2,1,0:T(8,128)(2,1)} %bitcast.273), channel_id=1, source_target_pairs={{0,64},{8,72},{16,80},{24,88},{32,96},{40,104},{48,112},{56,120},{... | collective-permute-start | bytes 786440 | tf_op jit(solution)/shard_map/ppermute | solution.py:16
  22.6 178.5 %collective-permute-start = (bf16[2,128,512]{2,1,0:T(8,128)(2,1)}, bf16[2,128,512]{2,1,0:T(8,128)(2,1)S(1)}, u32[]{:S(2)}, u32[]{:S(2)}) collective-permute-start(bf16[2,128,512]{2,1,0:T(8,128)(2,1)} %bitcast.281), channel_id=1, source_target_pairs={{0,8},{8,0},{16,24},{24,16},{32,40},{40,32},{48,56},{56,48},{64,72... | collective-permute-start | bytes 786440 | tf_op jit(solution)/shard_map/ppermute | solution.py:16
  28.1 240.0 %all-to-all-start = ((bf16[64,8,512]{2,1,0:T(8,128)(2,1)}), bf16[64,8,512]{2,1,0:T(8,128)(2,1)}, u32[]{:S(2)}, u32[]{:S(2)}) async-start(bf16[64,8,512]{2,1,0:T(8,128)(2,1)} %stack.2), calls=%async_computation | async-start | bytes 1048576 | tf_op jit(solution)/shard_map/all_to_all | solution.py:12
  39.5 281.4 %all-gather.2.cloned.1.call-start = ((), (), s32[]{:S(2)}) async-start(), calls=%async_computation.2 | async-start | bytes 4259840 | tf_op jit(solution)/shard_map/all_gather | solution.py:113
  40.3 361.4 %reduce-scatter.2.cloned.1.call-start = ((), (), s32[]{:S(2)}) async-start(), calls=%async_computation.3 | async-start | bytes 2359296 | tf_op jit(solution)/shard_map/reduce_scatter | solution.py:116
  184.7 19.1 %collective-permute-start.1 = (bf16[2,128,512]{2,1,0:T(8,128)(2,1)S(1)}, bf16[2,128,512]{2,1,0:T(8,128)(2,1)}, u32[]{:S(2)}, u32[]{:S(2)}) collective-permute-start(bf16[2,128,512]{2,1,0:T(8,128)(2,1)S(1)} %bitcast.275), channel_id=1, source_target_pairs={{0,8},{8,0},{16,24},{24,16},{32,40},{40,32},{48,56},{56,48},{64,72... | collective-permute-start | bytes 786440 | tf_op jit(solution)/shard_map/ppermute | solution.py:16
  186.7 40.4 %collective-permute-start.2 = (bf16[2,128,512]{2,1,0:T(8,128)(2,1)S(1)}, bf16[2,128,512]{2,1,0:T(8,128)(2,1)}, u32[]{:S(2)}, u32[]{:S(2)}) collective-permute-start(bf16[2,128,512]{2,1,0:T(8,128)(2,1)S(1)} %bitcast.283), channel_id=1, source_target_pairs={{0,16},{8,24},{16,0},{24,8},{32,48},{40,56},{48,32},{56,40},{64,80... | collective-permute-start | bytes 786440 | tf_op jit(solution)/shard_map/ppermute | solution.py:16
  191.9 43.2 %collective-permute-start.3 = (bf16[2,128,512]{2,1,0:T(8,128)(2,1)S(1)}, bf16[2,128,512]{2,1,0:T(8,128)(2,1)}, u32[]{:S(2)}, u32[]{:S(2)}) collective-permute-start(bf16[2,128,512]{2,1,0:T(8,128)(2,1)S(1)} %bitcast.276), channel_id=1, source_target_pairs={{0,16},{8,24},{16,0},{24,8},{32,48},{40,56},{48,32},{56,40},{64,80... | collective-permute-start | bytes 786440 | tf_op jit(solution)/shard_map/ppermute | solution.py:16
  197.3 40.1 %collective-permute-start.8 = (bf16[2,128,512]{2,1,0:T(8,128)(2,1)S(1)}, bf16[2,128,512]{2,1,0:T(8,128)(2,1)}, u32[]{:S(2)}, u32[]{:S(2)}) collective-permute-start(bf16[2,128,512]{2,1,0:T(8,128)(2,1)S(1)} %bitcast.284), channel_id=1, source_target_pairs={{0,128},{8,136},{16,144},{24,152},{32,160},{40,168},{48,176},{56,1... | collective-permute-start | bytes 786440 | tf_op jit(solution)/shard_map/ppermute | solution.py:16
  201.2 28.0 %copy-start.19 = (bf16[2,128,512]{2,1,0:T(8,128)(2,1)}, bf16[2,128,512]{2,1,0:T(8,128)(2,1)S(1)}, u32[]{:S(2)}) copy-start(bf16[2,128,512]{2,1,0:T(8,128)(2,1)S(1)} %collective-permute-done) | copy-start | bytes 786436
  201.2 37.7 %collective-permute-start.9 = (bf16[2,128,512]{2,1,0:T(8,128)(2,1)S(1)}, bf16[2,128,512]{2,1,0:T(8,128)(2,1)}, u32[]{:S(2)}, u32[]{:S(2)}) collective-permute-start(bf16[2,128,512]{2,1,0:T(8,128)(2,1)S(1)} %bitcast.277), channel_id=1, source_target_pairs={{0,128},{8,136},{16,144},{24,152},{32,160},{40,168},{48,176},{56,1... | collective-permute-start | bytes 786440 | tf_op jit(solution)/shard_map/ppermute | solution.py:16
  203.8 37.4 %collective-permute-start.11 = (bf16[2,128,512]{2,1,0:T(8,128)(2,1)S(1)}, bf16[2,128,512]{2,1,0:T(8,128)(2,1)}, u32[]{:S(2)}, u32[]{:S(2)}) collective-permute-start(bf16[2,128,512]{2,1,0:T(8,128)(2,1)S(1)} %bitcast.278), channel_id=1, source_target_pairs={{0,256},{8,264},{16,272},{24,280},{32,288},{40,296},{48,304},{56,3... | collective-permute-start | bytes 786440 | tf_op jit(solution)/shard_map/ppermute | solution.py:16
  227.1 16.2 %collective-permute-start.10 = (bf16[2,128,512]{2,1,0:T(8,128)(2,1)S(1)}, bf16[2,128,512]{2,1,0:T(8,128)(2,1)}, u32[]{:S(2)}, u32[]{:S(2)}) collective-permute-start(bf16[2,128,512]{2,1,0:T(8,128)(2,1)S(1)} %bitcast.285), channel_id=1, source_target_pairs={{0,256},{8,264},{16,272},{24,280},{32,288},{40,296},{48,304},{56,3... | collective-permute-start | bytes 786440 | tf_op jit(solution)/shard_map/ppermute | solution.py:16
  245.5 2.4 copy-start.13
  245.5 2.4 copy-start.14
  245.5 2.4 copy-start.15
  249.0 7.1 %copy-start.17 = (bf16[2,128,512]{2,1,0:T(8,128)(2,1)S(1)}, bf16[2,128,512]{2,1,0:T(8,128)(2,1)}, u32[]{:S(2)}) copy-start(bf16[2,128,512]{2,1,0:T(8,128)(2,1)} %get-tuple-element.82) | copy-start | bytes 786436
  249.0 7.9 %copy-start.16 = (bf16[2,128,512]{2,1,0:T(8,128)(2,1)S(1)}, bf16[2,128,512]{2,1,0:T(8,128)(2,1)}, u32[]{:S(2)}) copy-start(bf16[2,128,512]{2,1,0:T(8,128)(2,1)} %get-tuple-element.57) | copy-start | bytes 786436
  (11 other events, 14.4 us)
Sparse Core Ops, SparseCore 0:
  42.5 278.4 all-gather.1
  325.9 75.7 reduce-scatter.1
